TPU v7x, 32 devices: a whole 2x2x4 slice. The times are simulated.
32 devices in a mesh: dp: 8 (over y, x, core), tensor: 4 (over z).
Axes of the slice: x: 2, y: 2, z: 4, core: 2. Of those that a mesh axis runs over, the one named last changes fastest.
Arguments:
- layer_input: bfloat16 [32768, 768], P('dp'), may hold values from -6 to 6
- segments: int32 [32, 1024], P('dp'), may hold values from 0 to 7, never falling along the last dimension, each value on 1 to 512 neighbouring positions
- query_weight: bfloat16 [768, 768], P(None, 'tensor'), may hold values from -0.21875 to 0.21875
- query_bias: float32 [768], P('tensor'), may hold values from -3 to 3
- key_weight: bfloat16 [768, 768], P(None, 'tensor'), may hold values from -0.21875 to 0.21875
- value_weight: bfloat16 [768, 768], P(None, 'tensor'), may hold values from -0.21875 to 0.21875
- value_bias: float32 [768], P('tensor'), may hold values from -3 to 3
- output_weight: bfloat16 [768, 768], P('tensor'), may hold values from -0.875 to 0.875
- output_bias: float32 [768], replicated, may hold values from -3 to 3
- first_gain: float32 [768], replicated, may hold values from 0.5 to 1.5
- first_shift: float32 [768], replicated, may hold values from -3 to 3
- up_weight: bfloat16 [768, 3072], P(None, 'tensor'), may hold values from -0.21875 to 0.21875
- up_bias: float32 [3072], P('tensor'), may hold values from -3 to 3
- down_weight: bfloat16 [3072, 768], P('tensor'), may hold values from -0.109375 to 0.109375
- down_bias: float32 [768], replicated, may hold values from -3 to 3
- second_gain: float32 [768], replicated, may hold values from 0.5 to 1.5
- second_shift: float32 [768], replicated, may hold values from -3 to 3
- output_grad: bfloat16 [32768, 768], P('dp'), may hold values from -6 to 6
Outputs:
- layer_output: bfloat16 [32768, 768], P(('dp', 'tensor'))
- input_grad: float32 [32768, 768], P(('dp', 'tensor'))
- grad_query_weight: float32 [768, 768], P('dp', 'tensor')
- grad_query_bias: float32 [768], P('tensor')
- grad_key_weight: float32 [768, 768], P('dp', 'tensor')
- grad_value_weight: float32 [768, 768], P('dp', 'tensor')
- grad_value_bias: float32 [768], P('tensor')
- grad_output_weight: float32 [768, 768], P('tensor', 'dp')
- grad_output_bias: float32 [768], P(('dp', 'tensor'))
- grad_first_gain: float32 [768], P(('dp', 'tensor'))
- grad_first_shift: float32 [768], P(('dp', 'tensor'))
- grad_up_weight: float32 [768, 3072], P('dp', 'tensor')
- grad_up_bias: float32 [3072], P('tensor')
- grad_down_weight: float32 [3072, 768], P('tensor', 'dp')
- grad_down_bias: float32 [768], P(('dp', 'tensor'))
- grad_second_gain: float32 [768], P(('dp', 'tensor'))
- grad_second_shift: float32 [768], P(('dp', 'tensor'))
Inputs may be any that keep to these rules, and one draw needn't show every extreme that they name: `segments`: segment numbers restart in every packed row; a token attends exactly to the tokens of its own row that carry its segment number.
All inputs are finite; a program needn't handle non-finite values.
Results may differ from a plain program's by a relative error of at most 0.02.
The roundings to bfloat16 on the way count: a program that leaves them out, or rounds other values in their place, can miss the bound.
Values may be sent and summed in bfloat16 or wider, within the bound.
A program may use at most 256 MiB of HBM per device.

v0:
```python
import jax
import jax.numpy as jnp
from jax import lax
from jax.sharding import PartitionSpec as P

HEAD_DIM = 64
norm_eps = 1e-06


def product(left_side, right_side):
    return jnp.dot(left_side, right_side, preferred_element_type=jnp.float32)


def contract_rows(left_side, right_side):
    return lax.dot_general(
        left_side, right_side, (((0,), (0,)), ((), ())), preferred_element_type=jnp.float32
    )


def contract_last(left_side, right_side):
    return lax.dot_general(
        left_side, right_side, (((1,), (1,)), ((), ())), preferred_element_type=jnp.float32
    )


def normalize(summed, norm_gain, offset):
    centred = summed - jnp.mean(summed, -1, keepdims=True)
    inverse = lax.rsqrt(jnp.mean(centred * centred, -1, keepdims=True) + norm_eps)
    scaled = centred * inverse
    return (scaled * norm_gain + offset, scaled, inverse)


def normalize_back(grad_out, scaled, inverse, norm_gain):
    grad_scaled = grad_out * norm_gain
    mean_grad = jnp.mean(grad_scaled, -1, keepdims=True)
    mean_cross = jnp.mean(grad_scaled * scaled, -1, keepdims=True)
    return inverse * (grad_scaled - mean_grad - scaled * mean_cross)


def gelu_tanh(pre_act):
    return jax.nn.gelu(pre_act, approximate=True)


def score_block(query_block, key_row, query_segment, key_segment):
    scores = jnp.einsum(
        "qhd,khd->hqk", query_block, key_row, preferred_element_type=jnp.float32
    ) * HEAD_DIM ** (-0.5)
    linked = query_segment[:, None] == key_segment[None, :]
    return jnp.where(linked[None], scores, -1e30)


def attend(queries, key_side, value_proj, segments, block_rows):
    row_count, row_len = segments.shape
    head_count = queries.shape[1] // HEAD_DIM
    key_rows = key_side.reshape(row_count, row_len, head_count, HEAD_DIM)
    value_rows = value_proj.reshape(row_count, row_len, head_count, HEAD_DIM)
    block_count = row_count * row_len // block_rows
    query_blocks = queries.reshape(block_count, block_rows, head_count, HEAD_DIM)
    segment_blocks = segments.reshape(block_count, block_rows)
    row_ids = jnp.arange(block_count, dtype=jnp.int32) // (row_len // block_rows)

    def one_block(inputs):
        query_block, query_segment, row_id = inputs
        scores = score_block(query_block, key_rows[row_id], query_segment, segments[row_id])
        row_max = jnp.max(scores, -1, keepdims=True)
        exp_scores = jnp.exp(scores - row_max)
        row_total = jnp.sum(exp_scores, -1, keepdims=True)
        prob_low = (exp_scores / row_total).astype(jnp.bfloat16)
        context = jnp.einsum(
            "hqk,khd->qhd", prob_low, value_rows[row_id], preferred_element_type=jnp.float32
        )
        return (context.astype(jnp.bfloat16), (row_max + jnp.log(row_total))[..., 0])

    context, log_total = lax.map(one_block, (query_blocks, segment_blocks, row_ids))
    return (context.reshape(row_count * row_len, head_count * HEAD_DIM), log_total)


def attend_back(queries, key_side, value_proj, segments, log_total, grad_context, block_rows):
    row_count, row_len = segments.shape
    head_count = queries.shape[1] // HEAD_DIM
    local_width = head_count * HEAD_DIM
    key_rows = key_side.reshape(row_count, row_len, head_count, HEAD_DIM)
    value_rows = value_proj.reshape(row_count, row_len, head_count, HEAD_DIM)
    block_count = row_count * row_len // block_rows
    per_row = row_len // block_rows
    query_blocks = queries.reshape(block_count, block_rows, head_count, HEAD_DIM)
    grad_blocks = grad_context.reshape(block_count, block_rows, head_count, HEAD_DIM)
    segment_blocks = segments.reshape(block_count, block_rows)
    row_ids = jnp.arange(block_count, dtype=jnp.int32) // per_row

    def one_block(inputs):
        query_block, query_segment, row_id, log_block, grad_block = inputs
        scores = score_block(query_block, key_rows[row_id], query_segment, segments[row_id])
        probs_full = jnp.exp(scores - log_block[..., None])
        grad_probs = jnp.einsum(
            "qhd,khd->hqk", grad_block, value_rows[row_id], preferred_element_type=jnp.float32
        )
        inner_sum = jnp.sum(probs_full * grad_probs, -1, keepdims=True)
        grad_scores = (probs_full * (grad_probs - inner_sum)).astype(jnp.bfloat16)
        grad_query = jnp.einsum(
            "hqk,khd->qhd", grad_scores, key_rows[row_id], preferred_element_type=jnp.float32
        ) * HEAD_DIM ** (-0.5)
        grad_key = jnp.einsum(
            "hqk,qhd->khd", grad_scores, query_block, preferred_element_type=jnp.float32
        ) * HEAD_DIM ** (-0.5)
        grad_value = jnp.einsum(
            "hqk,qhd->khd",
            probs_full.astype(jnp.bfloat16),
            grad_block,
            preferred_element_type=jnp.float32,
        )
        return (grad_query, grad_key, grad_value)

    grad_query, grad_key, grad_value = lax.map(
        one_block, (query_blocks, segment_blocks, row_ids, log_total, grad_blocks)
    )
    grad_query = grad_query.reshape(row_count * row_len, local_width)
    grad_key = (
        grad_key.reshape(row_count, per_row, row_len, local_width)
        .sum(1)
        .reshape(row_count * row_len, local_width)
    )
    grad_value = (
        grad_value.reshape(row_count, per_row, row_len, local_width)
        .sum(1)
        .reshape(row_count * row_len, local_width)
    )
    return (grad_query, grad_key, grad_value)


def on_device(
    layer_input,
    segments,
    query_weight,
    query_bias,
    key_weight,
    value_weight,
    value_bias,
    output_weight,
    output_bias,
    first_gain,
    first_shift,
    up_weight,
    up_bias,
    down_weight,
    down_bias,
    second_gain,
    second_shift,
    output_grad,
):
    part_count = lax.axis_size("tensor")
    part_id = lax.axis_index("tensor")
    tok_count = layer_input.shape[0]
    share_rows = tok_count // part_count
    block_rows = min(512, segments.shape[1])

    def own_rows(full_array):
        return lax.dynamic_slice_in_dim(full_array, part_id * share_rows, share_rows, 0)

    input_f32 = layer_input.astype(jnp.float32)
    queries = (product(layer_input, query_weight) + query_bias).astype(jnp.bfloat16)
    key_side = product(layer_input, key_weight).astype(jnp.bfloat16)
    value_proj = (product(layer_input, value_weight) + value_bias).astype(jnp.bfloat16)
    context, log_total = attend(queries, key_side, value_proj, segments, block_rows)
    attn_total = lax.psum(product(context, output_weight).astype(jnp.bfloat16), "tensor").astype(
        jnp.float32
    )
    first_in = input_f32 + attn_total + output_bias
    first_out, first_unit, first_inv = normalize(first_in, first_gain, first_shift)
    first_low = first_out.astype(jnp.bfloat16)
    first_mine = own_rows(first_out)
    pre_act = product(first_low, up_weight) + up_bias
    gelu_out, pull_gelu = jax.vjp(gelu_tanh, pre_act)
    hidden_low = gelu_out.astype(jnp.bfloat16)
    down_mine = lax.psum_scatter(
        product(hidden_low, down_weight).astype(jnp.bfloat16),
        "tensor",
        scatter_dimension=0,
        tiled=True,
    ).astype(jnp.float32)
    second_in = first_mine + down_mine + down_bias
    second_out, second_unit, second_inv = normalize(second_in, second_gain, second_shift)
    layer_output = second_out.astype(jnp.bfloat16)
    grad_out_mine = own_rows(output_grad).astype(jnp.float32)
    grad_second = normalize_back(grad_out_mine, second_unit, second_inv, second_gain)
    grad_second_gain = jnp.sum(grad_out_mine * second_unit, 0)
    grad_second_shift = jnp.sum(grad_out_mine, 0)
    grad_down_bias = jnp.sum(grad_second, 0)
    down_low = lax.all_gather(grad_second.astype(jnp.bfloat16), "tensor", axis=0, tiled=True)
    grad_down_weight = contract_rows(hidden_low, down_low)
    grad_hidden = contract_last(down_low, down_weight)
    grad_pre = pull_gelu(grad_hidden)[0].astype(jnp.bfloat16)
    grad_up_weight = contract_rows(first_low, grad_pre)
    grad_up_bias = jnp.sum(grad_pre, 0, dtype=jnp.float32)
    up_back = contract_last(grad_pre, up_weight)
    mine_rows = own_rows(up_back) + grad_second
    first_grad = lax.psum(
        lax.dynamic_update_slice_in_dim(up_back, mine_rows, part_id * share_rows, 0).astype(
            jnp.bfloat16
        ),
        "tensor",
    ).astype(jnp.float32)
    attn_grad = normalize_back(first_grad, first_unit, first_inv, first_gain)
    attn_grad_low = attn_grad.astype(jnp.bfloat16)
    attn_grad_mine = own_rows(attn_grad)
    first_grad_mine = own_rows(first_grad)
    unit_mine = own_rows(first_unit)
    grad_first_gain = jnp.sum(first_grad_mine * unit_mine, 0)
    grad_first_shift = jnp.sum(first_grad_mine, 0)
    grad_output_bias = jnp.sum(attn_grad_mine, 0)
    grad_output_weight = contract_rows(context, attn_grad_low)
    grad_context = contract_last(attn_grad_low, output_weight).astype(jnp.bfloat16)
    grad_query, grad_key, grad_value = attend_back(
        queries, key_side, value_proj, segments, log_total, grad_context, block_rows
    )
    query_low = grad_query.astype(jnp.bfloat16)
    key_low = grad_key.astype(jnp.bfloat16)
    value_low = grad_value.astype(jnp.bfloat16)
    grad_query_weight = contract_rows(layer_input, query_low)
    grad_key_weight = contract_rows(layer_input, key_low)
    grad_value_weight = contract_rows(layer_input, value_low)
    grad_query_bias = jnp.sum(query_low, 0, dtype=jnp.float32)
    grad_value_bias = jnp.sum(value_low, 0, dtype=jnp.float32)
    total = contract_last(query_low, query_weight)
    total = total + contract_last(key_low, key_weight)
    input_grad = (
        lax.psum_scatter(
            (total + contract_last(value_low, value_weight)).astype(jnp.bfloat16),
            "tensor",
            scatter_dimension=0,
            tiled=True,
        ).astype(jnp.float32)
        + attn_grad_mine
    )
    summed_weights = (
        lax.psum_scatter(grad_query_weight, "dp", scatter_dimension=0, tiled=True),
        lax.psum_scatter(grad_key_weight, "dp", scatter_dimension=0, tiled=True),
        lax.psum_scatter(grad_value_weight, "dp", scatter_dimension=0, tiled=True),
        lax.psum_scatter(grad_up_weight, "dp", scatter_dimension=0, tiled=True),
        lax.psum_scatter(grad_output_weight, "dp", scatter_dimension=1, tiled=True),
        lax.psum_scatter(grad_down_weight, "dp", scatter_dimension=1, tiled=True),
    )
    summed_shared = (
        lax.psum_scatter(grad_output_bias, ("dp", "tensor"), scatter_dimension=0, tiled=True),
        lax.psum_scatter(grad_first_gain, ("dp", "tensor"), scatter_dimension=0, tiled=True),
        lax.psum_scatter(grad_first_shift, ("dp", "tensor"), scatter_dimension=0, tiled=True),
        lax.psum_scatter(grad_down_bias, ("dp", "tensor"), scatter_dimension=0, tiled=True),
        lax.psum_scatter(grad_second_gain, ("dp", "tensor"), scatter_dimension=0, tiled=True),
        lax.psum_scatter(grad_second_shift, ("dp", "tensor"), scatter_dimension=0, tiled=True),
    )
    summed_biases = lax.psum((grad_query_bias, grad_value_bias, grad_up_bias), "dp")
    return (
        layer_output,
        input_grad,
        summed_weights[0],
        summed_biases[0],
        summed_weights[1],
        summed_weights[2],
        summed_biases[1],
        summed_weights[4],
        summed_shared[0],
        summed_shared[1],
        summed_shared[2],
        summed_weights[3],
        summed_biases[2],
        summed_weights[5],
        summed_shared[3],
        summed_shared[4],
        summed_shared[5],
    )


def solution(mesh):
    in_specs = (
        P("dp", None),
        P("dp", None),
        P(None, "tensor"),
        P("tensor"),
        P(None, "tensor"),
        P(None, "tensor"),
        P("tensor"),
        P("tensor", None),
        P(),
        P(),
        P(),
        P(None, "tensor"),
        P("tensor"),
        P("tensor", None),
        P(),
        P(),
        P(),
        P("dp", None),
    )
    out_specs = (
        P(("dp", "tensor"), None),
        P(("dp", "tensor"), None),
        P("dp", "tensor"),
        P("tensor"),
        P("dp", "tensor"),
        P("dp", "tensor"),
        P("tensor"),
        P("tensor", "dp"),
        P(("dp", "tensor")),
        P(("dp", "tensor")),
        P(("dp", "tensor")),
        P("dp", "tensor"),
        P("tensor"),
        P("tensor", "dp"),
        P(("dp", "tensor")),
        P(("dp", "tensor")),
        P(("dp", "tensor")),
    )
    return jax.shard_map(
        on_device, mesh=mesh, in_specs=in_specs, out_specs=out_specs, check_vma=False
    )
```

profile of v0, /device:TPU:0, one launch (start us, length us, event | category | flops | bytes accessed | tf_op | source)
XLA Modules:
  0.0 1443.7 jit_solution(3081273717691375530)
XLA Ops:
  8.2 5.2 fusion.63
  24.1 5.0 convolution_convert_fusion.3
  33.3 86.0 %while.26 = (s32[]{:T(128)}, bf16[8,512,3,64]{1,3,2,0:T(8,128)(2,1)}, f32[8,3,512]{2,1,0:T(4,128)S(1)}, s32[8]{0:T(128)S(1)}, bf16[4,1024,3,64]{1,3,2,0:T(8,128)...) while((s32[]{:T(128)}, ...), condition=%wide.region_3.4_spmd, body=%wide.region_0.3_spmd.sunk | while | flops 422148608 | bytes 22225096 | solution.py:74
  40.3 3.7 fusion.142
  51.0 3.7 fusion.142
  61.8 3.7 fusion.142
  72.5 3.7 fusion.142
  83.3 3.7 fusion.142
  94.0 3.7 fusion.142
  104.8 3.7 fusion.142
  115.5 3.7 fusion.142
  123.9 4.5 convolution_convert_fusion
  128.7 225.5 %all-reduce.11.cloned.1.call-done = bf16[4096,768]{1,0:T(8,128)(2,1)} async-done(((bf16[4096,768]{1,0:T(8,128)(2,1)}), bf16[4096,768]{1,0:T(8,128)(2,1)}) %all-reduce.11.cloned.1.call-update) | async-done | bytes 6291472 | tf_op jit(solution)/shard_map/psum | solution.py:165
  354.2 6.9 fusion.61
  361.1 6.1 multiply_reduce_fusion.2
  367.3 6.1 multiply_add_fusion
  373.4 11.8 multiply_convert_fusion.1
  385.2 9.7 convolution_convert_fusion.1
  395.2 109.5 %reduce-scatter.17.cloned.1.call-done = bf16[1024,768]{1,0:T(8,128)(2,1)} async-done(((bf16[4096,768]{1,0:T(8,128)(2,1)}), bf16[1024,768]{1,0:T(8,128)(2,1)}) %reduce-scatter.17.cloned.1.call-update) | async-done | bytes 1572880 | tf_op jit(solution)/shard_map/reduce_scatter | solution.py:175
  511.5 4.0 fusion.81
  518.5 116.0 %all-gather.2.cloned.1.call-done = bf16[4096,768]{1,0:T(8,128)(2,1)} async-done(((bf16[1024,768]{1,0:T(8,128)(2,1)}), bf16[4096,768]{1,0:T(8,128)(2,1)}) %all-gather.2.cloned.1.call-update) | async-done | bytes 6291472 | tf_op jit(solution)/shard_map/all_gather | solution.py:189
  634.5 16.9 %convert_reduce_fusion = (f32[768]{0:T(1024)}, bf16[4096,768]{1,0:T(8,128)(2,1)S(1)}) fusion(f32[4096,768]{1,0:T(8,128)} %get-tuple-element.361, f32[768]{0:T(1024)S(1)} %copy-done.34, bf16[4096,768]{1,0:T(8,128)(2,1)} %all-gather.2.cloned.1.call-done, bf16[768,768]{1,0:T(8,128)(2,1)S(1)} %copy-done.33), kind=kOutput, calls=%fused_computation.74 | convolution fusion | flops 4904188928 | bytes 26351616 | tf_op jit(solution)/shard_map/dot_general | solution.py:21
  651.5 8.3 fusion.85
  659.8 4.3 add_dynamic-update-slice_fusion
  664.0 7.8 convert_element_type.120
  672.2 220.8 %all-reduce.13.cloned.1.call-done = bf16[4096,768]{1,0:T(8,128)(2,1)} async-done(((bf16[4096,768]{1,0:T(8,128)(2,1)}), bf16[4096,768]{1,0:T(8,128)(2,1)}) %all-reduce.13.cloned.1.call-update) | async-done | bytes 6291472 | tf_op jit(solution)/shard_map/psum | solution.py:197
  893.0 8.8 multiply_reduce_fusion.3
  901.8 7.9 subtract_multiply_fusion
  909.7 4.6 copy-done.2
  917.7 7.9 convolution_convert_fusion.2
  929.9 146.9 %while.27 = (s32[]{:T(128)}, bf16[8,512,3,64]{1,3,2,0:T(8,128)(2,1)}, f32[8,1024,3,64]{1,3,2,0:T(8,128)}, f32[8,1024,3,64]{1,3,2,0:T(8,128)}, s32[8]{0:T(128)S(1...) while((s32[]{:T(128)}, ...), condition=%wide.region_17.18_spmd, body=%wide.region_15.17_spmd.sunk | while | flops 1031043584 | bytes 53278952 | solution.py:114
  934.8 3.7 fusion.154
  938.5 3.6 multiply_reduce_fusion.7
  953.1 3.7 fusion.154
  956.8 3.6 multiply_reduce_fusion.7
  971.5 3.7 fusion.154
  975.2 3.6 multiply_reduce_fusion.7
  989.8 3.7 fusion.154
  993.5 3.6 multiply_reduce_fusion.7
  1008.1 3.7 fusion.154
  1011.9 3.6 multiply_reduce_fusion.7
  1026.5 3.7 fusion.154
  1030.2 3.6 multiply_reduce_fusion.7
  1044.9 3.7 fusion.154
  1063.2 3.7 fusion.154
  1076.8 4.0 reduce_sum.200
  1080.8 5.1 reduce_sum.199
  1091.2 6.4 fusion.87
  1097.6 6.3 fusion.86
  1103.9 12.8 add_convert_fusion
  1116.8 11.4 fusion.74
  1128.3 10.1 fusion.88
  1138.5 4.7 convolution_bitcast_fusion.2
  1144.4 4.7 convolution_bitcast_fusion.1
  1150.3 4.7 convolution_bitcast_fusion
  1158.0 8.3 convert_element_type.121
  1166.6 15.1 %all-reduce.7 = (f32[192]{0:T(256)}, f32[192]{0:T(256)}, f32[768]{0:T(1024)}) all-reduce(f32[192]{0:T(256)S(1)} %reduce_sum.202, f32[192]{0:T(256)S(1)} %convert_reduce_fusion.2, f32[768]{0:T(1024)S(1)} %copy-done.32), channel_id=1, replica_groups=mesh['dp'=8,'tensor'=4] {'dp'}, use_global_device_ids=true, to_apply=%region_23.24 | all-reduce | flops 1152 | bytes 9216 | tf_op jit(solution)/shard_map/psum | solution.py:251
  1186.7 40.0 %reduce-scatter.19.cloned.1.call-done = bf16[1024,768]{1,0:T(8,128)(2,1)} async-done(((bf16[4096,768]{1,0:T(8,128)(2,1)}), bf16[1024,768]{1,0:T(8,128)(2,1)}) %reduce-scatter.19.cloned.1.call-update) | async-done | bytes 1572880 | tf_op jit(solution)/shard_map/reduce_scatter | solution.py:227
  1226.6 4.4 dynamic-slice_reduce_fusion.1
  1231.0 41.2 %all-reduce.6 = (f32[768]{0:T(1024)S(1)}, f32[768]{0:T(1024)S(1)}, f32[768]{0:T(1024)S(1)}, f32[768]{0:T(1024)S(1)}, f32[768]{0:T(1024)S(1)}, /*index=5*/f32[768]{0:T(1024)S(1)}) all-reduce(f32[768]{0:T(1024)S(1)} %get-tuple-element.357, f32[768]{0:T(1024)S(1)} %get-tuple-element.287, ...), channel_id=8, replica_groups=mesh['dp'=8,'tensor'=4] {'dp','tensor'}, use_global_device_ids=true, to_apply=%region_30.31.clone | all-reduce | flops 4608 | bytes 36864
  1275.7 45.1 %reduce-scatter.23.cloned.1.call-done = f32[768,96]{0,1:T(8,128)} async-done(((f32[768,768]{0,1:T(8,128)}), f32[768,96]{0,1:T(8,128)}) %reduce-scatter.23.cloned.1.call-update) | async-done | bytes 294928 | tf_op jit(solution)/shard_map/reduce_scatter | solution.py:241
  1320.8 38.8 %reduce-scatter.25.cloned.1.call-done = f32[96,192]{1,0:T(8,128)} async-done(((f32[768,192]{1,0:T(8,128)}), f32[96,192]{1,0:T(8,128)}) %reduce-scatter.25.cloned.1.call-update) | async-done | bytes 73744
  1359.6 38.6 %reduce-scatter.27.cloned.1.call-done = f32[96,192]{1,0:T(8,128)} async-done(((f32[768,192]{1,0:T(8,128)}), f32[96,192]{1,0:T(8,128)}) %reduce-scatter.27.cloned.1.call-update) | async-done | bytes 73744
  1398.1 38.8 %reduce-scatter.29.cloned.1.call-done = f32[96,192]{1,0:T(8,128)} async-done(((f32[768,192]{1,0:T(8,128)}), f32[96,192]{1,0:T(8,128)}) %reduce-scatter.29.cloned.1.call-update) | async-done | bytes 73744
  (283 shorter events, 178.4 us)
Async XLA Ops:
  7.2 366.2 %copy-start = (bf16[768,768]{1,0:T(8,128)(2,1)S(1)}, bf16[768,768]{1,0:T(8,128)(2,1)}, u32[]{:S(2)}) copy-start(bf16[768,768]{1,0:T(8,128)(2,1)} %param.33) | copy-start | bytes 3538948
  7.2 347.0 %all-reduce.11.cloned.1.call-start = ((), (), s32[]{:S(2)}) async-start(), calls=%async_computation.8 | async-start | bytes 12582912 | tf_op jit(solution)/shard_map/psum | solution.py:165
  7.3 8.5 slice-start
  8.2 7.6 slice-start.1
  8.2 7.6 copy-start.17
  8.2 7.6 copy-start.35
  19.1 4.9 copy-start.19
  24.1 9.2 copy-start.22
  119.3 9.2 copy-start.6
  119.3 4.7 copy-start.16
  122.8 1.1 copy-start.11
  123.9 230.3 %copy-start.23 = (f32[768]{0:T(1024)S(1)}, f32[768]{0:T(1024)}, u32[]{:S(2)}) copy-start(f32[768]{0:T(1024)} %param.30) | copy-start | bytes 9220
  128.5 376.2 %reduce-scatter.17.cloned.1.call-start = ((), (), s32[]{:S(2)}) async-start(), calls=%async_computation.9 | async-start | bytes 7864320 | tf_op jit(solution)/shard_map/reduce_scatter | solution.py:175
  354.2 6.9 copy-start.4
  354.2 13.0 slice-start.2
  361.1 6.2 slice-start.3
  361.1 6.2 copy-start.5
  361.1 6.2 copy-start.24
  361.1 6.2 copy-start.30
  367.3 6.1 copy-start.34
  373.4 11.8 copy-start.3
  373.4 11.8 copy-start.33
  394.9 109.9 %copy-start.31 = (f32[768]{0:T(1024)S(1)}, f32[768]{0:T(1024)}, u32[]{:S(2)}) copy-start(f32[768]{0:T(1024)} %param.36) | copy-start | bytes 9220
  394.9 113.2 %copy-start.26 = (f32[768]{0:T(1024)S(1)}, f32[768]{0:T(1024)}, u32[]{:S(2)}) copy-start(f32[768]{0:T(1024)} %param.37) | copy-start | bytes 9220
  394.9 239.6 %all-gather.2.cloned.1.call-start = ((), (), s32[]{:S(2)}) async-start(), calls=%async_computation.10 | async-start | bytes 7864320 | tf_op jit(solution)/shard_map/all_gather | solution.py:189
  395.2 116.3 %copy-start.29 = (f32[768]{0:T(1024)S(1)}, f32[768]{0:T(1024)}, u32[]{:S(2)}) copy-start(f32[768]{0:T(1024)} %param.38) | copy-start | bytes 9220
  515.5 1.7 copy-start.8
  518.5 374.5 %all-reduce.13.cloned.1.call-start = ((), (), s32[]{:S(2)}) async-start(), calls=%async_computation.11 | async-start | bytes 12582912 | tf_op jit(solution)/shard_map/psum | solution.py:197
  651.5 8.3 copy-start.10
  651.5 8.3 copy-start.9
  671.8 513.2 %reduce-scatter.31.cloned.1.call-start = ((), (), s32[]{:S(2)}) async-start(), calls=%async_computation.18 | async-start | bytes 884736
  901.8 12.5 copy-start.12
  909.7 4.6 copy-start.2
  925.7 4.2 copy-start.7
  925.7 301.0 %reduce-scatter.19.cloned.1.call-start = ((), (), s32[]{:S(2)}) async-start(), calls=%async_computation.12 | async-start | bytes 7864320 | tf_op jit(solution)/shard_map/reduce_scatter | solution.py:227
  1085.9 5.3 copy-start.20
  1087.5 10.1 copy-start.13
  1091.0 6.6 copy-start.14
  1091.2 12.7 copy-start.15
  1091.2 6.4 copy-start.21
  1097.6 6.3 copy-start.18
  1116.8 158.9 %reduce-scatter.21.cloned.1.call-start = ((), (), s32[]{:S(2)}) async-start(), calls=%async_computation.13 | async-start | bytes 2654208 | tf_op jit(solution)/shard_map/reduce_scatter | solution.py:239
  1128.3 192.5 %reduce-scatter.23.cloned.1.call-start = ((), (), s32[]{:S(2)}) async-start(), calls=%async_computation.14 | async-start | bytes 2654208 | tf_op jit(solution)/shard_map/reduce_scatter | solution.py:241
  1138.4 221.1 %reduce-scatter.25.cloned.1.call-start = ((), (), s32[]{:S(2)}) async-start(), calls=%async_computation.15 | async-start | bytes 884736
  1144.3 253.8 %reduce-scatter.27.cloned.1.call-start = ((), (), s32[]{:S(2)}) async-start(), calls=%async_computation.16 | async-start | bytes 884736
  1150.2 286.7 %reduce-scatter.29.cloned.1.call-start = ((), (), s32[]{:S(2)}) async-start(), calls=%async_computation.17 | async-start | bytes 884736
  1158.0 8.6 copy-start.32
  1166.6 270.3 %copy-start.1 = (bf16[768,768]{1,0:T(8,128)(2,1)S(1)}, bf16[768,768]{1,0:T(8,128)(2,1)}, u32[]{:S(2)}) copy-start(bf16[768,768]{1,0:T(8,128)(2,1)} %param.33) | copy-start | bytes 3538948
  1181.7 49.3 %copy-start.25 = (f32[768]{0:T(1024)S(1)}, f32[768]{0:T(1024)}, u32[]{:S(2)}) copy-start(f32[768]{0:T(1024)} %get-tuple-element.345) | copy-start | bytes 9220
  1181.7 49.3 %copy-start.27 = (f32[768]{0:T(1024)S(1)}, f32[768]{0:T(1024)}, u32[]{:S(2)}) copy-start(f32[768]{0:T(1024)} %get-tuple-element.288) | copy-start | bytes 9220
  1181.7 49.3 %copy-start.28 = (f32[768]{0:T(1024)S(1)}, f32[768]{0:T(1024)}, u32[]{:S(2)}) copy-start(f32[768]{0:T(1024)} %get-tuple-element.293) | copy-start | bytes 9220
Sparse Core Ops, SparseCore 0:
  128.6 225.5 all-reduce.10
  395.0 109.6 reduce-scatter.16
  518.6 115.8 all-gather.1
  671.9 220.9 all-reduce.12
  925.8 33.9 reduce-scatter.30
  1116.9 109.6 reduce-scatter.18
  1230.6 43.4 reduce-scatter.20
  1278.3 42.4 reduce-scatter.22
  1324.5 34.9 reduce-scatter.24
  1363.1 34.9 reduce-scatter.26
  1401.9 34.9 reduce-scatter.28
where the time goes:
time: 1450 us; the launch traced here: 1440 us
  waiting for transfers between devices  873 us (60%)
  matrix products  294 us (20%)
  other arithmetic  121 us (8%)
  blocking collectives  56.3 us (4%)
  local copies, waits for them, and re-layouts  50.9 us (4%)
  loops' own time  31.9 us (2%)
  between operations  14.7 us (1%)
    psum x1, waiting for transfers between devices, on_device(): lax.psum(product(context, output_weight).astype(jnp.bfloat16), 'tensor')  225 us
    psum x1, waiting for transfers between devices, on_device(): lax.psum(lax.dynamic_update_slice_in_dim(up_back, mine_rows, part_id * sh...  221 us
    unnamed x15, waiting for transfers between devices  116 us
    all_gather x1, waiting for transfers between devices, on_device(): lax.all_gather(grad_second.astype(jnp.bfloat16), 'tensor', axis=0, tiled=...  116 us
    reduce_scatter x1, waiting for transfers between devices, on_device(): lax.psum_scatter(product(hidden_low, down_weight).astype(jnp.bfloat16), '...  110 us
    dot_general x6, matrix products, contract_last(): lax.dot_general(left_side, right_side, (((1,), (1,)), ((), ())), preferre...  58.7 us
    reduce_scatter x1, waiting for transfers between devices, on_device(): lax.psum_scatter(grad_down_weight, 'dp', scatter_dimension=1, tiled=True)  45.1 us
    unnamed x1, blocking collectives  41.2 us
  transfers between devices with their start and end apart: 11, of which 9 were waited for; matrix products, arithmetic and copies ran while one was open for 16% of the time, Pallas kernels for 0%

commit v1 on v0

--- a/solution.py
+++ b/solution.py
@@ -5,6 +5,18 @@
 
 HEAD_DIM = 64
 norm_eps = 1e-06
+
+
+def collect(x, axis, dim):
+    ways, here, step = (lax.axis_size(axis), lax.axis_index(axis), x.shape[dim])
+    line, have = (x, 1)
+    while have < ways:
+        line = jnp.concatenate(
+            [line, lax.ppermute(line, axis, [(d, (d - have) % ways) for d in range(ways)])],
+            axis=dim,
+        )
+        have = 2 * have
+    return jnp.roll(line, here * step, axis=dim)
 
 
 def product(left_side, right_side):
@@ -186,7 +198,7 @@
     grad_second_gain = jnp.sum(grad_out_mine * second_unit, 0)
     grad_second_shift = jnp.sum(grad_out_mine, 0)
     grad_down_bias = jnp.sum(grad_second, 0)
-    down_low = lax.all_gather(grad_second.astype(jnp.bfloat16), "tensor", axis=0, tiled=True)
+    down_low = collect(grad_second.astype(jnp.bfloat16), "tensor", 0)
     grad_down_weight = contract_rows(hidden_low, down_low)
     grad_hidden = contract_last(down_low, down_weight)
     grad_pre = pull_gelu(grad_hidden)[0].astype(jnp.bfloat16)

time: 1450 us -> 1520 us (1.048)
  waiting for transfers between devices: 873 us -> 924 us
  local copies, waits for them, and re-layouts: 50.9 us -> 66.3 us
    ppermute x0 -> x2, waiting for transfers between devices: none -> 168 us  [collect(): lax.ppermute(line, axis, [(d, (d - have) % ways) for d in range(ways)])]
    all_gather x1 -> x0, waiting for transfers between devices: 116 us -> none  [on_device(): lax.all_gather(grad_second.astype(jnp.bfloat16), 'tensor', axis=0, tiled=...]
    unnamed x94 -> x104, local copies, waits for them, and re-layouts: 20.2 us -> 32.2 us
    unnamed x15 -> x14, waiting for transfers between devices: 116 us -> 116 us
  transfers between devices with their start and end apart: 11 -> 12, of which waited for: 9 -> 10; matrix products, arithmetic and copies ran while one was open for 16% -> 16% of each run, Pallas kernels for 0% -> 0%
where the time goes in v1:
time: 1520 us
  waiting for transfers between devices  924 us (61%)
  matrix products  294 us (19%)
  other arithmetic  123 us (8%)
  local copies, waits for them, and re-layouts  66.3 us (4%)
  blocking collectives  55.5 us (4%)
  loops' own time  32.2 us (2%)
    psum x1, waiting for transfers between devices, on_device(): lax.psum(product(context, output_weight).astype(jnp.bfloat16), 'tensor')  226 us
    psum x1, waiting for transfers between devices, on_device(): lax.psum(lax.dynamic_update_slice_in_dim(up_back, mine_rows, part_id * sh...  224 us
    ppermute x2, waiting for transfers between devices, collect(): lax.ppermute(line, axis, [(d, (d - have) % ways) for d in range(ways)])  168 us
    unnamed x14, waiting for transfers between devices  116 us
    reduce_scatter x1, waiting for transfers between devices, on_device(): lax.psum_scatter(product(hidden_low, down_weight).astype(jnp.bfloat16), '...  110 us
    dot_general x6, matrix products, contract_last(): lax.dot_general(left_side, right_side, (((1,), (1,)), ((), ())), preferre...  58.4 us
    reduce_scatter x1, waiting for transfers between devices, on_device(): lax.psum_scatter(grad_down_weight, 'dp', scatter_dimension=1, tiled=True)  45.1 us
    unnamed x1, blocking collectives  41.2 us
  transfers between devices with their start and end apart: 12, of which 10 were waited for; matrix products, arithmetic and copies ran while one was open for 16% of the time, Pallas kernels for 0%

profile of v1, /device:TPU:0, one launch (start us, length us, event | category | flops | bytes accessed | tf_op | source)
XLA Modules:
  0.0 1516.5 jit_solution(6222977816128036728)
XLA Ops:
  8.2 5.2 fusion.67
  23.8 5.0 convolution_convert_fusion.3
  33.0 86.0 %while.26 = (s32[]{:T(128)}, bf16[8,512,3,64]{1,3,2,0:T(8,128)(2,1)}, f32[8,3,512]{2,1,0:T(4,128)S(1)}, s32[8]{0:T(128)S(1)}, bf16[4,1024,3,64]{1,3,2,0:T(8,128)...) while((s32[]{:T(128)}, ...), condition=%wide.region_3.4_spmd, body=%wide.region_0.3_spmd.sunk | while | flops 422148608 | bytes 22225096 | solution.py:86
  40.0 3.7 fusion.143
  50.7 3.7 fusion.143
  61.5 3.7 fusion.143
  72.2 3.7 fusion.143
  83.0 3.7 fusion.143
  93.7 3.7 fusion.143
  104.5 3.7 fusion.143
  115.2 3.7 fusion.143
  123.6 4.5 convolution_convert_fusion
  128.3 225.7 %all-reduce.11.cloned.1.call-done = bf16[4096,768]{1,0:T(8,128)(2,1)} async-done(((bf16[4096,768]{1,0:T(8,128)(2,1)}), bf16[4096,768]{1,0:T(8,128)(2,1)}) %all-reduce.11.cloned.1.call-update) | async-done | bytes 6291472 | tf_op jit(solution)/shard_map/psum | solution.py:177
  353.9 6.9 fusion.61
  360.8 5.7 multiply_reduce_fusion.2
  366.6 6.1 multiply_add_fusion
  372.7 7.3 fusion.80
  380.0 4.5 copy-done.38
  384.4 9.8 convolution_convert_fusion.1
  394.3 109.8 %reduce-scatter.17.cloned.1.call-done = bf16[1024,768]{1,0:T(8,128)(2,1)} async-done(((bf16[4096,768]{1,0:T(8,128)(2,1)}), bf16[1024,768]{1,0:T(8,128)(2,1)}) %reduce-scatter.17.cloned.1.call-update) | async-done | bytes 1572880 | tf_op jit(solution)/shard_map/reduce_scatter | solution.py:187
  507.5 3.8 fusion.74
  511.3 4.0 fusion.87
  520.8 33.8 %collective-permute-done = bf16[1024,768]{1,0:T(8,128)(2,1)S(1)} collective-permute-done((bf16[1024,768]{1,0:T(8,128)(2,1)S(1)}, bf16[1024,768]{1,0:T(8,128)(2,1)S(1)}, u32[]{:S(2)}, u32[]{:S(2)}) %collective-permute-start) | collective-permute-done | bytes 1572896 | tf_op jit(solution)/shard_map/ppermute | solution.py:15
  560.5 133.9 %collective-permute-done.1 = bf16[2048,768]{1,0:T(8,128)(2,1)} collective-permute-done((bf16[2048,768]{1,0:T(8,128)(2,1)}, bf16[2048,768]{1,0:T(8,128)(2,1)}, u32[]{:S(2)}, u32[]{:S(2)}) %collective-permute-start.1) | collective-permute-done | bytes 3145760 | tf_op jit(solution)/shard_map/ppermute | solution.py:15
  694.3 3.7 constant_dynamic-update-slice_fusion.3
  700.6 3.7 constant_dynamic-update-slice_fusion
  704.3 17.0 %convert_reduce_fusion = (f32[768]{0:T(1024)}, bf16[4096,768]{1,0:T(8,128)(2,1)S(1)}) fusion(f32[4096,768]{1,0:T(8,128)} %copy-done.38, f32[768]{0:T(1024)S(1)} %copy-done.35, bf16[768,768]{1,0:T(8,128)(2,1)S(1)} %copy-done, bf16[8192,768]{1,0:T(8,128)(2,1)} %constant_dynamic-update-slice_fusion, s32[]{:T(128)S(6)} %select_n.51), kind=kOutput, calls=%fused_computation.74 | convolution fusion | flops 4904188928 | bytes 26351620 | tf_op jit(solution)/shard_map/dot_general | solution.py:33
  721.3 8.0 fusion.91
  729.3 4.2 add_dynamic-update-slice_fusion
  733.5 7.9 convert_element_type.120
  741.7 223.8 %all-reduce.13.cloned.1.call-done = bf16[4096,768]{1,0:T(8,128)(2,1)} async-done(((bf16[4096,768]{1,0:T(8,128)(2,1)}), bf16[4096,768]{1,0:T(8,128)(2,1)}) %all-reduce.13.cloned.1.call-update) | async-done | bytes 6291472 | tf_op jit(solution)/shard_map/psum | solution.py:209
  965.5 8.8 multiply_reduce_fusion.3
  974.3 7.9 subtract_multiply_fusion
  982.2 4.4 copy-done.2
  990.1 7.9 convolution_convert_fusion.2
  1002.1 147.3 %while.27 = (s32[]{:T(128)}, bf16[8,512,3,64]{1,3,2,0:T(8,128)(2,1)}, f32[8,1024,3,64]{1,3,2,0:T(8,128)}, f32[8,1024,3,64]{1,3,2,0:T(8,128)}, s32[8]{0:T(128)S(1...) while((s32[]{:T(128)}, ...), condition=%wide.region_17.18_spmd, body=%wide.region_15.17_spmd.sunk | while | flops 1031043584 | bytes 53278952 | solution.py:126
  1007.0 3.7 fusion.155
  1025.4 3.7 fusion.155
  1043.7 3.7 fusion.155
  1047.4 3.6 multiply_reduce_fusion.7
  1062.1 3.7 fusion.155
  1080.4 3.8 fusion.155
  1098.9 3.7 fusion.155
  1117.2 3.7 fusion.155
  1135.5 3.7 fusion.155
  1149.4 4.0 reduce_sum.200
  1153.4 5.1 reduce_sum.199
  1163.8 6.4 fusion.93
  1170.2 6.3 fusion.92
  1176.6 12.8 add_convert_fusion
  1189.4 11.4 fusion.78
  1201.0 14.4 fusion.62
  1215.4 4.7 convolution_bitcast_fusion.2
  1221.3 4.8 convolution_bitcast_fusion.1
  1227.6 4.7 convolution_bitcast_fusion
  1235.2 8.3 convert_element_type.121
  1243.8 14.3 all-reduce.7
  1263.1 36.2 %reduce-scatter.19.cloned.1.call-done = bf16[1024,768]{1,0:T(8,128)(2,1)} async-done(((bf16[4096,768]{1,0:T(8,128)(2,1)}), bf16[1024,768]{1,0:T(8,128)(2,1)}) %reduce-scatter.19.cloned.1.call-update) | async-done | bytes 1572880 | tf_op jit(solution)/shard_map/reduce_scatter | solution.py:239
  1299.2 4.4 dynamic-slice_reduce_fusion.1
  1303.6 41.2 %all-reduce.6 = (f32[768]{0:T(1024)S(1)}, f32[768]{0:T(1024)S(1)}, f32[768]{0:T(1024)S(1)}, f32[768]{0:T(1024)S(1)}, f32[768]{0:T(1024)S(1)}, /*index=5*/f32[768]{0:T(1024)S(1)}) all-reduce(f32[768]{0:T(1024)S(1)} %get-tuple-element.359, f32[768]{0:T(1024)S(1)} %get-tuple-element.287, ...), channel_id=8, replica_groups=mesh['dp'=8,'tensor'=4] {'dp','tensor'}, use_global_device_ids=true, to_apply=%region_30.31.clone | all-reduce | flops 4608 | bytes 36864
  1348.3 45.1 %reduce-scatter.23.cloned.1.call-done = f32[768,96]{0,1:T(8,128)} async-done(((f32[768,768]{0,1:T(8,128)}), f32[768,96]{0,1:T(8,128)}) %reduce-scatter.23.cloned.1.call-update) | async-done | bytes 294928 | tf_op jit(solution)/shard_map/reduce_scatter | solution.py:253
  1393.4 38.7 %reduce-scatter.25.cloned.1.call-done = f32[96,192]{1,0:T(8,128)} async-done(((f32[768,192]{1,0:T(8,128)}), f32[96,192]{1,0:T(8,128)}) %reduce-scatter.25.cloned.1.call-update) | async-done | bytes 73744
  1432.1 38.8 %reduce-scatter.27.cloned.1.call-done = f32[96,192]{1,0:T(8,128)} async-done(((f32[768,192]{1,0:T(8,128)}), f32[96,192]{1,0:T(8,128)}) %reduce-scatter.27.cloned.1.call-update) | async-done | bytes 73744
  1470.8 38.6 %reduce-scatter.29.cloned.1.call-done = f32[96,192]{1,0:T(8,128)} async-done(((f32[768,192]{1,0:T(8,128)}), f32[96,192]{1,0:T(8,128)}) %reduce-scatter.29.cloned.1.call-update) | async-done | bytes 73744
  (296 shorter events, 203.1 us)
Async XLA Ops:
  7.2 377.3 %copy-start = (bf16[768,768]{1,0:T(8,128)(2,1)S(1)}, bf16[768,768]{1,0:T(8,128)(2,1)}, u32[]{:S(2)}) copy-start(bf16[768,768]{1,0:T(8,128)(2,1)} %param.35) | copy-start | bytes 3538948
  7.2 346.7 %all-reduce.11.cloned.1.call-start = ((), (), s32[]{:S(2)}) async-start(), calls=%async_computation.8 | async-start | bytes 12582912 | tf_op jit(solution)/shard_map/psum | solution.py:177
  7.3 8.5 slice-start
  8.2 7.6 slice-start.1
  8.2 7.6 copy-start.18
  8.2 7.6 copy-start.37
  19.1 4.7 copy-start.20
  23.8 9.2 copy-start.23
  119.0 9.2 copy-start.5
  119.0 4.7 copy-start.17
  122.5 1.2 copy-start.10
  123.6 230.3 %copy-start.24 = (f32[768]{0:T(1024)S(1)}, f32[768]{0:T(1024)}, u32[]{:S(2)}) copy-start(f32[768]{0:T(1024)} %param.30) | copy-start | bytes 9220
  128.2 375.9 %reduce-scatter.17.cloned.1.call-start = ((), (), s32[]{:S(2)}) async-start(), calls=%async_computation.9 | async-start | bytes 7864320 | tf_op jit(solution)/shard_map/reduce_scatter | solution.py:187
  353.9 6.9 copy-start.4
  353.9 12.7 slice-start.2
  360.8 5.8 slice-start.3
  360.8 5.8 copy-start.25
  360.8 5.8 copy-start.31
  372.7 7.3 copy-start.3
  372.7 11.8 copy-start.35
  380.0 4.5 copy-start.38
  394.2 109.9 %copy-start.32 = (f32[768]{0:T(1024)S(1)}, f32[768]{0:T(1024)}, u32[]{:S(2)}) copy-start(f32[768]{0:T(1024)} %param.36) | copy-start | bytes 9220
  394.3 113.2 %copy-start.27 = (f32[768]{0:T(1024)S(1)}, f32[768]{0:T(1024)}, u32[]{:S(2)}) copy-start(f32[768]{0:T(1024)} %param.37) | copy-start | bytes 9220
  394.3 571.2 %all-reduce.13.cloned.1.call-start = ((), (), s32[]{:S(2)}) async-start(), calls=%async_computation.10 | async-start | bytes 12582912 | tf_op jit(solution)/shard_map/psum | solution.py:209
  394.3 116.9 %copy-start.30 = (f32[768]{0:T(1024)S(1)}, f32[768]{0:T(1024)}, u32[]{:S(2)}) copy-start(f32[768]{0:T(1024)} %param.38) | copy-start | bytes 9220
  515.2 1.6 copy-start.7
  518.2 36.4 %copy-start.12 = (bf16[1024,768]{1,0:T(8,128)(2,1)}, bf16[1024,768]{1,0:T(8,128)(2,1)S(1)}, u32[]{:S(2)}) copy-start(bf16[1024,768]{1,0:T(8,128)(2,1)S(1)} %get-tuple-element.350) | copy-start | bytes 4718596
  518.2 36.4 %collective-permute-start = (bf16[1024,768]{1,0:T(8,128)(2,1)S(1)}, bf16[1024,768]{1,0:T(8,128)(2,1)S(1)}, u32[]{:S(2)}, u32[]{:S(2)}) collective-permute-start(bf16[1024,768]{1,0:T(8,128)(2,1)S(1)} %get-tuple-element.350), channel_id=1, source_target_pairs={{0,3},{1,0},{2,1},{3,2},{4,7},{5,4},{6,5},{7,6},{8,11},{9,8},{10,9... | collective-permute-start | bytes 4718600 | tf_op jit(solution)/shard_map/ppermute | solution.py:15
  556.5 137.8 %collective-permute-start.1 = (bf16[2048,768]{1,0:T(8,128)(2,1)}, bf16[2048,768]{1,0:T(8,128)(2,1)}, u32[]{:S(2)}, u32[]{:S(2)}) collective-permute-start(bf16[2048,768]{1,0:T(8,128)(2,1)} %pad_maximum_fusion), channel_id=1, source_target_pairs={{0,2},{1,3},{2,0},{3,1},{4,6},{5,7},{6,4},{7,5},{8,10},{9,11},{10,... | collective-permute-start | bytes 9437192 | tf_op jit(solution)/shard_map/ppermute | solution.py:15
  559.2 138.9 %copy-start.13 = (bf16[1024,768]{1,0:T(8,128)(2,1)S(1)}, bf16[1024,768]{1,0:T(8,128)(2,1)}, u32[]{:S(2)}) copy-start(bf16[1024,768]{1,0:T(8,128)(2,1)} %copy-done.12) | copy-start | bytes 4718596
  704.3 17.0 %copy-start.34 = (bf16[768,768]{1,0:T(8,128)(2,1)S(1)}, bf16[768,768]{1,0:T(8,128)(2,1)}, u32[]{:S(2)}) copy-start(bf16[768,768]{1,0:T(8,128)(2,1)} %param.33) | copy-start | bytes 3538948
  721.3 8.0 copy-start.9
  721.3 8.0 copy-start.8
  741.4 520.0 %reduce-scatter.31.cloned.1.call-start = ((), (), s32[]{:S(2)}) async-start(), calls=%async_computation.17 | async-start | bytes 884736
  974.3 12.3 copy-start.11
  982.2 4.4 copy-start.2
  998.0 4.1 copy-start.6
  998.0 301.2 %reduce-scatter.19.cloned.1.call-start = ((), (), s32[]{:S(2)}) async-start(), calls=%async_computation.11 | async-start | bytes 7864320 | tf_op jit(solution)/shard_map/reduce_scatter | solution.py:239
  1158.5 5.3 copy-start.21
  1160.1 10.1 copy-start.14
  1163.6 6.6 copy-start.15
  1163.8 12.8 copy-start.16
  1163.8 6.4 copy-start.22
  1170.2 6.3 copy-start.19
  1189.4 11.6 copy-start.36
  1189.4 158.9 %reduce-scatter.21.cloned.1.call-start = ((), (), s32[]{:S(2)}) async-start(), calls=%async_computation.12 | async-start | bytes 2654208 | tf_op jit(solution)/shard_map/reduce_scatter | solution.py:251
  1200.9 192.5 %reduce-scatter.23.cloned.1.call-start = ((), (), s32[]{:S(2)}) async-start(), calls=%async_computation.13 | async-start | bytes 2654208 | tf_op jit(solution)/shard_map/reduce_scatter | solution.py:253
  1215.4 216.7 %reduce-scatter.25.cloned.1.call-start = ((), (), s32[]{:S(2)}) async-start(), calls=%async_computation.14 | async-start | bytes 884736
  1221.3 249.6 %reduce-scatter.27.cloned.1.call-start = ((), (), s32[]{:S(2)}) async-start(), calls=%async_computation.15 | async-start | bytes 884736
  1227.3 282.1 %reduce-scatter.29.cloned.1.call-start = ((), (), s32[]{:S(2)}) async-start(), calls=%async_computation.16 | async-start | bytes 884736
  1235.2 8.6 copy-start.33
  1243.8 265.6 %copy-start.1 = (bf16[768,768]{1,0:T(8,128)(2,1)S(1)}, bf16[768,768]{1,0:T(8,128)(2,1)}, u32[]{:S(2)}) copy-start(bf16[768,768]{1,0:T(8,128)(2,1)} %param.35) | copy-start | bytes 3538948
  1258.2 45.4 %copy-start.26 = (f32[768]{0:T(1024)S(1)}, f32[768]{0:T(1024)}, u32[]{:S(2)}) copy-start(f32[768]{0:T(1024)} %get-tuple-element.345) | copy-start | bytes 9220
  1258.2 45.4 %copy-start.28 = (f32[768]{0:T(1024)S(1)}, f32[768]{0:T(1024)}, u32[]{:S(2)}) copy-start(f32[768]{0:T(1024)} %get-tuple-element.288) | copy-start | bytes 9220
  1258.2 45.4 %copy-start.29 = (f32[768]{0:T(1024)S(1)}, f32[768]{0:T(1024)}, u32[]{:S(2)}) copy-start(f32[768]{0:T(1024)} %get-tuple-element.293) | copy-start | bytes 9220
Sparse Core Ops, SparseCore 0:
  128.3 225.5 all-reduce.10
  394.4 109.6 reduce-scatter.16
  741.6 223.8 all-reduce.12
  998.1 33.9 reduce-scatter.30
  1189.5 109.7 reduce-scatter.18
  1303.0 43.4 reduce-scatter.20
  1350.8 42.4 reduce-scatter.22
  1397.1 34.9 reduce-scatter.24
  1435.8 34.9 reduce-scatter.26
  1474.4 34.9 reduce-scatter.28
